TPU v7x, 32 devices: a whole 2x2x4 slice. The times are simulated.
32 devices in a mesh: dp: 4 (over y, x), tensor: 8 (over z, core).
Axes of the slice: x: 2, y: 2, z: 4, core: 2. Of those that a mesh axis runs over, the one named last changes fastest.
Arguments:
- activations: bfloat16 [1024, 16384], P('dp', 'tensor'), may hold values from -6 to 6
- angles: float32 [14, 8192], P(None, 'tensor'), may hold values from -3.140625 to 3.140625
- clip_bits: int32 [64, 16384], P('dp', 'tensor'), may hold values from 0 to 65535, as said below
- codes: bfloat16 [16384, 10240], P('tensor', 'dp'), may hold values from -127 to 127, as said below
- exponents: int32 [10240], replicated, may hold values from -16 to -13
- cotangent: bfloat16 [1024, 10240], P('dp', 'tensor'), may hold values from -6 to 6
Outputs:
- input_grad: bfloat16 [1024, 16384], P('dp', 'tensor')
- angle_grad: float32 [14, 8192], P(None, 'tensor')
Inputs may be any that keep to these rules, and one draw needn't show every extreme that they name: Bit k (0 to 15) of clip_bits[w, i] is the clip mask of token 16 w + k at feature i; higher bits are zero. `codes`: every entry is a whole number.
All inputs are finite; a program needn't handle non-finite values.
Results may differ from a plain program's by a relative error of at most 0.003.
Values may be sent and summed in bfloat16 or wider, within the bound.
No kernel may reach another device: no remote copies, remote signals or barrier semaphores. Data moves between devices by JAX's collectives and lax.ppermute only.
A program may use at most 128 MiB of HBM per device.

v0:
```python
import jax
import jax.numpy as jnp
from jax import lax
from jax.sharding import PartitionSpec as P


def partner(value, axis, apart):
    mask = 2**apart
    pairs = [(source, source ^ mask) for source in range(lax.axis_size(axis))]
    return lax.ppermute(value, axis, pairs)


def unpack_mask(clip_bits, rows, width):
    shifts = jnp.arange(16, dtype=jnp.int32)
    bits = jnp.bitwise_and(jnp.right_shift(clip_bits[:, None, :], shifts[None, :, None]), 1)
    return bits.reshape(rows, width).astype(jnp.float32)


def section_terms(table, section, first, width):
    half = 1 << section
    index = first + jnp.arange(width, dtype=jnp.int32)
    pair = jnp.right_shift(index, section + 1) * half + jnp.bitwise_and(index, half - 1)
    theta = jnp.take(table[section], pair)
    lower = jnp.bitwise_and(index, half) == 0
    sign = jnp.where(lower, -1.0, 1.0).astype(jnp.float32)
    return (jnp.cos(theta), sign * jnp.sin(theta), sign, pair)


def local_partner(field, section):
    half = 1 << section
    column = jnp.arange(field.shape[1], dtype=jnp.int32)
    lower = jnp.bitwise_and(column, half) == 0
    return jnp.where(lower[None, :], jnp.roll(field, -half, axis=1), jnp.roll(field, half, axis=1))


def scatter_terms(term, pair, half_pairs):
    return jnp.zeros((half_pairs,), jnp.float32).at[pair].add(term)


def body(activations, angles, clip_bits, codes, exponents, cotangent):
    rows, width = activations.shape
    sections = angles.shape[0]
    share = angles.shape[1]
    half_pairs = share * lax.axis_size("tensor")
    local_count = width.bit_length() - 1
    place = lax.axis_index("tensor")
    table = lax.all_gather(angles, "tensor", axis=1, tiled=True)
    scale = jnp.exp2(exponents.astype(jnp.float32))
    full_cot = lax.all_gather(cotangent, "tensor", axis=1, tiled=True)
    weight_piece = (
        lax.all_gather(codes, "dp", axis=1, tiled=True).astype(jnp.float32) * scale[None, :]
    ).astype(jnp.bfloat16)
    projected = lax.dot_general(
        full_cot, weight_piece, (((1,), (1,)), ((), ())), preferred_element_type=jnp.float32
    )
    grad_rot = projected * unpack_mask(clip_bits, rows, width)
    first = place * width
    field = activations.astype(jnp.float32)
    stored = [None] * sections
    for section in range(sections):
        cosine, signed, sign, pair = section_terms(table, section, first, width)
        if section < local_count:
            other = local_partner(field, section)
        else:
            other = partner(field.astype(jnp.bfloat16), "tensor", section - local_count).astype(
                field.dtype
            )
            stored[section] = (field, other)
        field = cosine * field + signed * other
    grad = grad_rot
    terms_list = [None] * sections
    for section in reversed(range(sections)):
        cosine, signed, sign, pair = section_terms(table, section, first, width)
        if section < local_count:
            other = local_partner(field, section)
            grad_other = local_partner(grad, section)
            before = cosine * field - signed * other
        else:
            before, before_other = stored[section]
            other = cosine * before_other - signed * before
            grad_other = partner(grad, "tensor", section - local_count)
        terms_list[section] = scatter_terms(jnp.sum(sign * grad * other, axis=0), pair, half_pairs)
        grad = cosine * grad - signed * grad_other
        field = before
    input_grad = grad.astype(jnp.bfloat16)
    collected = jnp.stack(terms_list)
    partial_total = lax.psum_scatter(collected, "tensor", scatter_dimension=1, tiled=True)
    angle_grad = lax.psum(partial_total, "dp")
    return (input_grad, angle_grad)


def solution(mesh):
    placed = (
        P("dp", "tensor"),
        P(None, "tensor"),
        P("dp", "tensor"),
        P("tensor", "dp"),
        P(),
        P("dp", "tensor"),
    )
    return jax.shard_map(
        body,
        mesh=mesh,
        in_specs=placed,
        out_specs=(P("dp", "tensor"), P(None, "tensor")),
        check_vma=False,
    )
```

profile of v0, /device:TPU:0, one launch (start us, length us, event | category | flops | bytes accessed | tf_op | source)
XLA Modules:
  0.0 975.6 jit_solution(11110099458539859929)
XLA Ops:
  11.8 18.1 %all_gather.9 = f32[14,8192]{1,0:T(8,128)S(1)} all-gather(f32[14,1024]{1,0:T(8,128)S(1)} %copy-done.17), channel_id=1, replica_groups=mesh['dp'=4,'tensor'=8] {'tensor'}, dimensions={1}, use_global_device_ids=true | all-gather | bytes 516096 | tf_op jit(solution)/shard_map/all_gather | solution.py:47
  30.3 11.8 %gather_fusion = f32[2048]{0:T(1024)S(1)} fusion(f32[8192]{0:T(1024)S(1)} %bitcast.61, s32[2048]{0:T(1024)S(1)} %get-tuple-element.217), kind=kCustom, calls=%fused_computation.clone | custom fusion | bytes 24576 | tf_op jit(solution)/shard_map/jit(_take)/gather | solution.py:23
  42.1 11.8 %gather_fusion.1 = f32[2048]{0:T(1024)S(1)} fusion(f32[8192]{0:T(1024)S(1)} %bitcast.60, s32[2048]{0:T(1024)S(1)} %get-tuple-element.230), kind=kCustom, calls=%fused_computation.1.clone | custom fusion | bytes 24576 | tf_op jit(solution)/shard_map/jit(_take)/gather | solution.py:23
  53.9 11.8 %gather_fusion.2 = f32[2048]{0:T(1024)S(1)} fusion(f32[8192]{0:T(1024)S(1)} %bitcast.59, s32[2048]{0:T(1024)S(1)} %get-tuple-element.218), kind=kCustom, calls=%fused_computation.2.clone | custom fusion | bytes 24576 | tf_op jit(solution)/shard_map/jit(_take)/gather | solution.py:23
  65.7 11.8 %gather_fusion.3 = f32[2048]{0:T(1024)S(1)} fusion(f32[8192]{0:T(1024)S(1)} %bitcast.58, s32[2048]{0:T(1024)S(1)} %get-tuple-element.219), kind=kCustom, calls=%fused_computation.3.clone | custom fusion | bytes 24576 | tf_op jit(solution)/shard_map/jit(_take)/gather | solution.py:23
  77.5 11.8 %gather_fusion.4 = f32[2048]{0:T(1024)S(1)} fusion(f32[8192]{0:T(1024)S(1)} %bitcast.57, s32[2048]{0:T(1024)S(1)} %get-tuple-element.220), kind=kCustom, calls=%fused_computation.4.clone | custom fusion | bytes 24576 | tf_op jit(solution)/shard_map/jit(_take)/gather | solution.py:23
  89.3 11.8 %gather_fusion.5 = f32[2048]{0:T(1024)S(1)} fusion(f32[8192]{0:T(1024)S(1)} %bitcast.56, s32[2048]{0:T(1024)S(1)} %get-tuple-element.221), kind=kCustom, calls=%fused_computation.5.clone | custom fusion | bytes 24576 | tf_op jit(solution)/shard_map/jit(_take)/gather | solution.py:23
  101.1 11.8 %gather_fusion.6 = f32[2048]{0:T(1024)S(1)} fusion(f32[8192]{0:T(1024)S(1)} %bitcast.55, s32[2048]{0:T(1024)S(1)} %get-tuple-element.222), kind=kCustom, calls=%fused_computation.6.clone | custom fusion | bytes 24576 | tf_op jit(solution)/shard_map/jit(_take)/gather | solution.py:23
  112.9 11.8 %gather_fusion.7 = f32[2048]{0:T(1024)S(1)} fusion(f32[8192]{0:T(1024)S(1)} %bitcast.54, s32[2048]{0:T(1024)S(1)} %get-tuple-element.223), kind=kCustom, calls=%fused_computation.7.clone | custom fusion | bytes 24576 | tf_op jit(solution)/shard_map/jit(_take)/gather | solution.py:23
  124.7 11.8 %gather_fusion.8 = f32[2048]{0:T(1024)S(1)} fusion(f32[8192]{0:T(1024)S(1)} %bitcast.53, s32[2048]{0:T(1024)S(1)} %get-tuple-element.224), kind=kCustom, calls=%fused_computation.8.clone | custom fusion | bytes 24576 | tf_op jit(solution)/shard_map/jit(_take)/gather | solution.py:23
  136.5 11.8 %gather_fusion.9 = f32[2048]{0:T(1024)S(1)} fusion(f32[8192]{0:T(1024)S(1)} %bitcast.52, s32[2048]{0:T(1024)S(1)} %get-tuple-element.225), kind=kCustom, calls=%fused_computation.9.clone | custom fusion | bytes 24576 | tf_op jit(solution)/shard_map/jit(_take)/gather | solution.py:23
  148.3 11.8 %gather_fusion.10 = f32[2048]{0:T(1024)S(1)} fusion(f32[8192]{0:T(1024)S(1)} %bitcast.51, s32[2048]{0:T(1024)S(1)} %get-tuple-element.226), kind=kCustom, calls=%fused_computation.10.clone | custom fusion | bytes 24576 | tf_op jit(solution)/shard_map/jit(_take)/gather | solution.py:23
  189.1 249.2 %all-gather.3.cloned.1.call-done = bf16[2048,10240]{1,0:T(8,128)(2,1)} async-done(((bf16[2048,2560]{1,0:T(8,128)(2,1)}), bf16[2048,10240]{1,0:T(8,128)(2,1)}) %all-gather.3.cloned.1.call-update) | async-done | bytes 41943056 | tf_op jit(solution)/shard_map/all_gather | solution.py:51
  438.3 20.5 %fusion.3 = f32[256,2048]{0,1:T(8,128)} fusion(bf16[256,10240]{1,0:T(8,128)(2,1)} %all-gather.5.cloned.1.call-done, bf16[2048,10240]{1,0:T(8,128)(2,1)} %all-gather.3.cloned.1.call-done, f32[10240]{0:T(1024)S(1)} %multiply_exponential_fusion, s32[256,2048]{0,1:T(8,128)S(1)} %copy-done.2, s32[256]{0:T(256)S(1)} %shift_right_arithmetic.224), kind=kOutput, calls=%fused_computation.32 | convolution fusion | flops 10802429952 | bytes 51422208 | tf_op jit(solution)/shard_map/dot_general | solution.py:53
  464.3 11.8 %gather_fusion.11 = f32[2048]{0:T(1024)S(1)} fusion(f32[8192]{0:T(1024)S(1)} %bitcast.50, s32[2048]{0:T(1024)S(1)} %get-tuple-element.227), kind=kCustom, calls=%fused_computation.11.clone | custom fusion | bytes 24576 | tf_op jit(solution)/shard_map/jit(_take)/gather | solution.py:23
  476.1 11.8 %gather_fusion.13 = f32[2048]{0:T(1024)S(1)} fusion(f32[8192]{0:T(1024)S(1)} %bitcast.49, s32[2048]{0:T(1024)S(1)} %get-tuple-element.229), kind=kCustom, calls=%fused_computation.13.clone | custom fusion | bytes 24576 | tf_op jit(solution)/shard_map/jit(_take)/gather | solution.py:23
  491.0 61.3 %collective-permute-done = f32[256,2048]{0,1:T(8,128)} collective-permute-done((f32[256,2048]{0,1:T(8,128)}, f32[256,2048]{0,1:T(8,128)}, u32[]{:S(2)}, u32[]{:S(2)}) %collective-permute-start) | collective-permute-done | bytes 2097184 | tf_op jit(solution)/shard_map/ppermute | solution.py:10
  552.4 3.5 multiply_subtract_fusion.12
  556.3 11.8 %gather_fusion.12 = f32[2048]{0:T(1024)S(1)} fusion(f32[8192]{0:T(1024)S(1)} %bitcast.48, s32[2048]{0:T(1024)S(1)} %get-tuple-element.228), kind=kCustom, calls=%fused_computation.12.clone | custom fusion | bytes 24576 | tf_op jit(solution)/shard_map/jit(_take)/gather | solution.py:23
  568.1 3.1 fusion.57
  571.2 3.5 collective-permute-start.5
  574.9 49.2 %collective-permute-done.5 = bf16[256,2048]{0,1:T(8,128)(2,1)S(1)} collective-permute-done((bf16[256,2048]{0,1:T(8,128)(2,1)S(1)}, bf16[256,2048]{0,1:T(8,128)(2,1)S(1)}, u32[]{:S(2)}, u32[]{:S(2)}) %collective-permute-start.5) | collective-permute-done | bytes 1048608 | tf_op jit(solution)/shard_map/ppermute | solution.py:10
  626.8 8.2 multiply_reduce_fusion
  640.0 14.7 %scatter_custom_fusion.13 = f32[8192]{0:T(1024)S(1)} fusion(s32[2048]{0:T(1024)S(1)} %bitcast.90, f32[2048]{0:T(1024)S(1)} %get-tuple-element.7, f32[]{:T(128)} %constant.42.clone.1), kind=kCustom, calls=%fused_computation.177 | custom fusion | flops 2048 | bytes 32772 | tf_op jit(solution)/shard_map/scatter-add | solution.py:37
  654.7 14.7 %scatter_custom_fusion.12 = f32[8192]{0:T(1024)S(1)} fusion(s32[2048]{0:T(1024)S(1)} %bitcast.89, f32[2048]{0:T(1024)S(1)} %get-tuple-element.8, f32[]{:T(128)} %constant.42.clone.1), kind=kCustom, calls=%fused_computation.179 | custom fusion | flops 2048 | bytes 32772 | tf_op jit(solution)/shard_map/scatter-add | solution.py:37
  669.4 14.7 %scatter_custom_fusion.11 = f32[8192]{0:T(1024)S(1)} fusion(s32[2048]{0:T(1024)S(1)} %bitcast.88, f32[2048]{0:T(1024)S(1)} %get-tuple-element.9, f32[]{:T(128)} %constant.42.clone.1), kind=kCustom, calls=%fused_computation.181 | custom fusion | flops 2048 | bytes 32772 | tf_op jit(solution)/shard_map/scatter-add | solution.py:37
  684.2 4.7 multiply_reduce_fusion.1
  689.4 3.9 multiply_reduce_fusion.2
  696.3 3.9 multiply_reduce_fusion.3
  703.2 3.4 multiply_reduce_fusion.4
  709.5 3.2 multiply_reduce_fusion.5
  715.4 3.1 multiply_reduce_fusion.6
  721.4 3.2 multiply_reduce_fusion.7
  742.1 3.2 multiply_reduce_fusion.10
  747.6 14.9 %scatter_custom_fusion.10 = f32[8192]{0:T(1024)S(1)} fusion(s32[2048]{0:T(1024)} %bitcast.83, f32[2048]{0:T(1024)S(1)} %get-tuple-element.13, f32[]{:T(128)} %constant.42.clone.1), kind=kCustom, calls=%fused_computation.183 | custom fusion | flops 2048 | bytes 33280 | tf_op jit(solution)/shard_map/scatter-add | solution.py:37
  762.5 14.9 %scatter_custom_fusion.9 = f32[8192]{0:T(1024)S(1)} fusion(s32[2048]{0:T(1024)} %bitcast.86, f32[2048]{0:T(1024)S(1)} %get-tuple-element.15, f32[]{:T(128)} %constant.42.clone.1), kind=kCustom, calls=%fused_computation.185 | custom fusion | flops 2048 | bytes 33280 | tf_op jit(solution)/shard_map/scatter-add | solution.py:37
  777.3 14.9 %scatter_custom_fusion.8 = f32[8192]{0:T(1024)S(1)} fusion(s32[2048]{0:T(1024)} %bitcast.84, f32[2048]{0:T(1024)S(1)} %get-tuple-element.17, f32[]{:T(128)} %constant.42.clone.1), kind=kCustom, calls=%fused_computation.187 | custom fusion | flops 2048 | bytes 33280 | tf_op jit(solution)/shard_map/scatter-add | solution.py:37
  792.2 14.9 %scatter_custom_fusion.7 = f32[8192]{0:T(1024)S(1)} fusion(s32[2048]{0:T(1024)} %bitcast.87, f32[2048]{0:T(1024)S(1)} %get-tuple-element.19, f32[]{:T(128)} %constant.42.clone.1), kind=kCustom, calls=%fused_computation.189 | custom fusion | flops 2048 | bytes 33280 | tf_op jit(solution)/shard_map/scatter-add | solution.py:37
  807.1 15.1 %scatter_custom_fusion.6 = f32[8192]{0:T(1024)S(1)} fusion(s32[2048]{0:T(1024)} %bitcast.85, f32[2048]{0:T(1024)S(1)} %get-tuple-element.21, f32[]{:T(128)} %constant.42.clone.1), kind=kCustom, calls=%fused_computation.191 | custom fusion | flops 2048 | bytes 33280 | tf_op jit(solution)/shard_map/scatter-add | solution.py:37
  822.2 14.9 %scatter_custom_fusion.5 = f32[8192]{0:T(1024)S(1)} fusion(s32[2048]{0:T(1024)} %bitcast.82, f32[2048]{0:T(1024)S(1)} %get-tuple-element.23, f32[]{:T(128)} %constant.42.clone.1), kind=kCustom, calls=%fused_computation.193 | custom fusion | flops 2048 | bytes 33280 | tf_op jit(solution)/shard_map/scatter-add | solution.py:37
  837.1 14.9 %scatter_custom_fusion.4 = f32[8192]{0:T(1024)S(1)} fusion(s32[2048]{0:T(1024)} %bitcast.80, f32[2048]{0:T(1024)S(1)} %get-tuple-element.25, f32[]{:T(128)} %constant.42.clone.1), kind=kCustom, calls=%fused_computation.195 | custom fusion | flops 2048 | bytes 33280 | tf_op jit(solution)/shard_map/scatter-add | solution.py:37
  851.9 14.9 %scatter_custom_fusion.3 = f32[8192]{0:T(1024)S(1)} fusion(s32[2048]{0:T(1024)} %bitcast.81, f32[2048]{0:T(1024)S(1)} %get-tuple-element.27, f32[]{:T(128)} %constant.42.clone.1), kind=kCustom, calls=%fused_computation.197 | custom fusion | flops 2048 | bytes 33280 | tf_op jit(solution)/shard_map/scatter-add | solution.py:37
  866.8 14.9 %scatter_custom_fusion.2 = f32[8192]{0:T(1024)S(1)} fusion(s32[2048]{0:T(1024)} %bitcast.79, f32[2048]{0:T(1024)S(1)} %get-tuple-element.29, f32[]{:T(128)} %constant.42.clone.1), kind=kCustom, calls=%fused_computation.199 | custom fusion | flops 2048 | bytes 33280 | tf_op jit(solution)/shard_map/scatter-add | solution.py:37
  881.6 14.9 %scatter_custom_fusion.1 = f32[8192]{0:T(1024)S(1)} fusion(s32[2048]{0:T(1024)} %bitcast.78, f32[2048]{0:T(1024)S(1)} %get-tuple-element.31, f32[]{:T(128)} %constant.42.clone.1), kind=kCustom, calls=%fused_computation.201 | custom fusion | flops 2048 | bytes 33280 | tf_op jit(solution)/shard_map/scatter-add | solution.py:37
  896.5 6.4 fusion.56
  902.9 14.9 %scatter_custom_fusion = f32[8192]{0:T(1024)S(1)} fusion(s32[2048]{0:T(1024)} %bitcast.77, f32[2048]{0:T(1024)S(1)} %get-tuple-element.33, f32[]{:T(128)} %constant.42.clone.1), kind=kCustom, calls=%fused_computation.203 | custom fusion | flops 2048 | bytes 33280 | tf_op jit(solution)/shard_map/scatter-add | solution.py:37
  926.3 24.4 %reduce-scatter.2.cloned.1.call-done = f32[14,1024]{1,0:T(8,128)} async-done(((f32[14,8192]{1,0:T(8,128)}), f32[14,1024]{1,0:T(8,128)}) %reduce-scatter.2.cloned.1.call-update) | async-done | bytes 57360 | tf_op jit(solution)/shard_map/reduce_scatter | solution.py:87
  950.7 17.9 %psum.7 = f32[14,1024]{1,0:T(8,128)} all-reduce(f32[14,1024]{1,0:T(8,128)} %reduce-scatter.2.cloned.1.call-done), channel_id=1, replica_groups=mesh['dp'=4,'tensor'=8] {'dp'}, use_global_device_ids=true, to_apply=%region_29.31 | all-reduce | flops 14336 | bytes 114688 | tf_op jit(solution)/shard_map/psum | solution.py:88
  (204 shorter events, 93.2 us)
Async XLA Ops:
  7.2 181.9 %all-gather.5.cloned.1.call-start = ((), (), s32[]{:S(2)}) async-start(), calls=%async_computation.2 | async-start | bytes 5898240 | tf_op jit(solution)/shard_map/all_gather | solution.py:49
  7.9 1.2 copy-start.3
  7.9 430.4 %all-gather.3.cloned.1.call-start = ((), (), s32[]{:S(2)}) async-start(), calls=%async_computation.1 | async-start | bytes 52428800 | tf_op jit(solution)/shard_map/all_gather | solution.py:51
  8.7 1.0 copy-start.4
  8.7 942.0 %reduce-scatter.2.cloned.1.call-start = ((), (), s32[]{:S(2)}) async-start(), calls=%async_computation.3 | async-start | bytes 589824 | tf_op jit(solution)/shard_map/reduce_scatter | solution.py:87
  9.9 1.9 copy-start.17
  160.1 6.8 copy-start.20
  160.2 0.6 copy-start.23
  160.2 3.3 copy-start.18
  160.3 0.6 copy-start.13
  160.3 0.6 copy-start.15
  163.2 0.6 copy-start.5
  163.2 0.6 copy-start.7
  166.5 0.6 copy-start.9
  166.6 0.6 copy-start.11
  187.4 1.7 copy-start.1
  187.4 1.7 copy-start.22
  187.4 250.9 %copy-start.2 = (s32[256,2048]{0,1:T(8,128)S(1)}, s32[256,2048]{0,1:T(8,128)}, u32[]{:S(2)}) copy-start(s32[256,2048]{0,1:T(8,128)} %copy.11) | copy-start | bytes 6291460
  458.9 93.5 %collective-permute-start = (f32[256,2048]{0,1:T(8,128)}, f32[256,2048]{0,1:T(8,128)}, u32[]{:S(2)}, u32[]{:S(2)}) collective-permute-start(f32[256,2048]{0,1:T(8,128)} %fusion.3), channel_id=1, source_target_pairs={{0,4},{1,5},{2,6},{3,7},{4,0},{5,1},{6,2},{7,3},{8,12},{9,13},{10,... | collective-permute-start | bytes 6291464 | tf_op jit(solution)/shard_map/ppermute | solution.py:10
  464.3 23.7 %collective-permute-start.3 = (bf16[256,2048]{0,1:T(8,128)(2,1)}, bf16[256,2048]{0,1:T(8,128)(2,1)S(1)}, u32[]{:S(2)}, u32[]{:S(2)}) collective-permute-start(bf16[256,2048]{0,1:T(8,128)(2,1)} %get-tuple-element.11), channel_id=1, source_target_pairs={{0,1},{1,0},{2,3},{3,2},{4,5},{5,4},{6,7},{7,6},{8,9},{9,8},{10,11... | collective-permute-start | bytes 3145736 | tf_op jit(solution)/shard_map/ppermute | solution.py:10
  489.5 78.6 %collective-permute-start.4 = (bf16[256,2048]{0,1:T(8,128)(2,1)}, bf16[256,2048]{0,1:T(8,128)(2,1)}, u32[]{:S(2)}, u32[]{:S(2)}) collective-permute-start(bf16[256,2048]{0,1:T(8,128)(2,1)} %fusion.182), channel_id=1, source_target_pairs={{0,2},{1,3},{2,0},{3,1},{4,6},{5,7},{6,4},{7,5},{8,10},{9,11},{10,... | collective-permute-start | bytes 3145736 | tf_op jit(solution)/shard_map/ppermute | solution.py:10
  555.8 70.9 %collective-permute-start.1 = (f32[256,2048]{0,1:T(8,128)}, f32[256,2048]{0,1:T(8,128)}, u32[]{:S(2)}, u32[]{:S(2)}) collective-permute-start(f32[256,2048]{0,1:T(8,128)} %multiply_subtract_fusion.12), channel_id=1, source_target_pairs={{0,2},{1,3},{2,0},{3,1},{4,6},{5,7},{6,4},{7,5},{8,10},{9,11},{10,... | collective-permute-start | bytes 6291464 | tf_op jit(solution)/shard_map/ppermute | solution.py:10
  571.2 52.8 %collective-permute-start.5 = (bf16[256,2048]{0,1:T(8,128)(2,1)S(1)}, bf16[256,2048]{0,1:T(8,128)(2,1)S(1)}, u32[]{:S(2)}, u32[]{:S(2)}) collective-permute-start(bf16[256,2048]{0,1:T(8,128)(2,1)S(1)} %fusion.57), channel_id=1, source_target_pairs={{0,4},{1,5},{2,6},{3,7},{4,0},{5,1},{6,2},{7,3},{8,12},{9,13},{10,... | collective-permute-start | bytes 3145736 | tf_op jit(solution)/shard_map/ppermute | solution.py:10
  635.0 49.2 %collective-permute-start.2 = (f32[256,2048]{0,1:T(8,128)}, f32[256,2048]{0,1:T(8,128)}, u32[]{:S(2)}, u32[]{:S(2)}) collective-permute-start(f32[256,2048]{0,1:T(8,128)} %get-tuple-element.10), channel_id=1, source_target_pairs={{0,1},{1,0},{2,3},{3,2},{4,5},{5,4},{6,7},{7,6},{8,9},{9,8},{10,11... | collective-permute-start | bytes 6291464 | tf_op jit(solution)/shard_map/ppermute | solution.py:10
  730.3 0.7 copy-start.10
  730.3 0.7 copy-start.12
  730.3 0.7 copy-start.21
  736.7 0.7 copy-start.6
  736.7 0.7 copy-start.8
  736.7 0.7 copy-start.19
  745.3 151.2 %copy-start.24 = (pred[2048]{0:T(1024)(128)(4,1)S(1)}, pred[2048]{0:T(1024)(128)(4,1)}, u32[]{:S(2)}) copy-start(pred[2048]{0:T(1024)(128)(4,1)} %copy-done.23) | copy-start | bytes 6148
  919.9 2.9 copy-start
  919.9 2.9 copy-start.14
  919.9 2.8 copy-start.16
Sparse Core Ops, SparseCore 0:
  9.6 60.3 all-gather.4
  71.8 366.4 all-gather.2
  920.0 30.6 reduce-scatter.1
where the time goes:
time: 986 us; the launch traced here: 976 us
  waiting for transfers between devices  388 us (39%)
  other arithmetic  315 us (32%)
  local copies, waits for them, and re-layouts  193 us (20%)
  blocking collectives  36.1 us (4%)
  matrix products  20.5 us (2%)
  between operations  15.6 us (2%)
    all_gather x1, waiting for transfers between devices, body(): lax.all_gather(codes, 'dp', axis=1, tiled=True).astype(jnp.float32)  249 us
    scatter-add x14, other arithmetic, scatter_terms(): return jnp.zeros((half_pairs,), jnp.float32).at[pair].add(term)  208 us
    gather x14, local copies, waits for them, and re-layouts, section_terms(): theta = jnp.take(table[section], pair)  165 us
    ppermute x6, waiting for transfers between devices, partner(): return lax.ppermute(value, axis, pairs)  113 us
    reduce_sum x12, other arithmetic, body(): jnp.sum(sign * grad * other, axis=0)  49 us
    reduce_scatter x1, waiting for transfers between devices, body(): lax.psum_scatter(collected, 'tensor', scatter_dimension=1, tiled=True)  24.4 us
    add x10, other arithmetic, body(): field = cosine * field + signed * other  22.2 us
    dot_general x1, matrix products, body(): lax.dot_general(full_cot, weight_piece, (((1,), (1,)), ((), ())), preferr...  20.5 us
  transfers between devices with their start and end apart: 9, of which 5 were waited for; matrix products, arithmetic and copies ran while one was open for 27% of the time, Pallas kernels for 0%

commit v1 on v0

--- a/solution.py
+++ b/solution.py
@@ -2,6 +2,18 @@
 import jax.numpy as jnp
 from jax import lax
 from jax.sharding import PartitionSpec as P
+
+
+def collect(shard, axis, dim):
+    ways, here = (lax.axis_size(axis), lax.axis_index(axis))
+    grown, reach = (shard, 1)
+    while reach < ways:
+        theirs = lax.ppermute(grown, axis, [(d, d ^ reach) for d in range(ways)])
+        mine_first = jnp.concatenate([grown, theirs], axis=dim)
+        theirs_first = jnp.concatenate([theirs, grown], axis=dim)
+        grown = jnp.where(here & reach == 0, mine_first, theirs_first)
+        reach = 2 * reach
+    return grown
 
 
 def partner(value, axis, apart):
@@ -47,9 +59,9 @@
     table = lax.all_gather(angles, "tensor", axis=1, tiled=True)
     scale = jnp.exp2(exponents.astype(jnp.float32))
     full_cot = lax.all_gather(cotangent, "tensor", axis=1, tiled=True)
-    weight_piece = (
-        lax.all_gather(codes, "dp", axis=1, tiled=True).astype(jnp.float32) * scale[None, :]
-    ).astype(jnp.bfloat16)
+    weight_piece = (collect(codes, "dp", 1).astype(jnp.float32) * scale[None, :]).astype(
+        jnp.bfloat16
+    )
     projected = lax.dot_general(
         full_cot, weight_piece, (((1,), (1,)), ((), ())), preferred_element_type=jnp.float32
     )

time: 986 us -> 1260 us (1.28)
  waiting for transfers between devices: 388 us -> 634 us
  matrix products: 20.5 us -> 38.8 us
  other arithmetic: 315 us -> 330 us
    ppermute x0 -> x2, waiting for transfers between devices: none -> 494 us  [collect(): theirs = lax.ppermute(grown, axis, [(d, d ^ reach) for d in range(ways)])]
    all_gather x1 -> x0, waiting for transfers between devices: 249 us -> none  [body(): lax.all_gather(codes, 'dp', axis=1, tiled=True).astype(jnp.float32)]
    select_n x0 -> x1, other arithmetic: none -> 22.1 us  [collect(): grown = jnp.where(here & reach == 0, mine_first, theirs_first)]
    dot_general x1, matrix products: 20.5 us -> 38.8 us  [body(): lax.dot_general(full_cot, weight_piece, (((1,), (1,)), ((), ())), preferr...]
  transfers between devices with their start and end apart: 9 -> 10, of which waited for: 5 -> 6; matrix products, arithmetic and copies ran while one was open for 27% -> 21% of each run, Pallas kernels for 0% -> 0%
where the time goes in v1:
time: 1260 us
  waiting for transfers between devices  634 us (50%)
  other arithmetic  330 us (26%)
  local copies, waits for them, and re-layouts  192 us (15%)
  matrix products  38.8 us (3%)
  blocking collectives  34.2 us (3%)
  between operations  16.1 us (1%)
  starting transfers between devices  12.9 us (1%)
    ppermute x2, waiting for transfers between devices, collect(): theirs = lax.ppermute(grown, axis, [(d, d ^ reach) for d in range(ways)])  494 us
    scatter-add x14, other arithmetic, scatter_terms(): return jnp.zeros((half_pairs,), jnp.float32).at[pair].add(term)  207 us
    gather x14, local copies, waits for them, and re-layouts, section_terms(): theta = jnp.take(table[section], pair)  165 us
    ppermute x6, waiting for transfers between devices, partner(): return lax.ppermute(value, axis, pairs)  113 us
    reduce_sum x12, other arithmetic, body(): jnp.sum(sign * grad * other, axis=0)  45.7 us
    dot_general x1, matrix products, body(): lax.dot_general(full_cot, weight_piece, (((1,), (1,)), ((), ())), preferr...  38.8 us
    reduce_scatter x1, waiting for transfers between devices, body(): lax.psum_scatter(collected, 'tensor', scatter_dimension=1, tiled=True)  27.1 us
  transfers between devices with their start and end apart: 10, of which 6 were waited for; matrix products, arithmetic and copies ran while one was open for 21% of the time, Pallas kernels for 0%

profile of v1, /device:TPU:0, one launch (start us, length us, event | category | flops | bytes accessed | tf_op | source)
XLA Modules:
  0.0 1258.3 jit_solution(15353627693217996631)
XLA Ops:
  10.2 225.7 %collective-permute-done = bf16[2048,2560]{1,0:T(8,128)(2,1)} collective-permute-done((bf16[2048,2560]{1,0:T(8,128)(2,1)}, bf16[2048,2560]{1,0:T(8,128)(2,1)}, u32[]{:S(2)}, u32[]{:S(2)}) %collective-permute-start) | collective-permute-done | bytes 10485792 | tf_op jit(solution)/shard_map/ppermute | solution.py:11
  236.0 22.1 %maximum_select_fusion.2 = bf16[2048,5120]{1,0:T(8,128)(2,1)} fusion(bf16[2048,2560]{1,0:T(8,128)(2,1)} %collective-permute-done, bf16[2048,2560]{1,0:T(8,128)(2,1)} %param.11, pred[]{:T(512)S(6)} %eq.251), kind=kLoop, calls=%fused_computation.38 | loop fusion | flops 94371840 | bytes 41943040 | tf_op jit(solution)/shard_map/jit(_where)/select_n | solution.py:14
  260.5 16.2 %all_gather.6 = f32[14,8192]{1,0:T(8,128)S(1)} all-gather(f32[14,1024]{1,0:T(8,128)S(1)} %copy-done.29), channel_id=1, replica_groups=mesh['dp'=4,'tensor'=8] {'tensor'}, dimensions={1}, use_global_device_ids=true | all-gather | bytes 516096 | tf_op jit(solution)/shard_map/all_gather | solution.py:59
  277.7 12.0 gather_fusion
  289.7 11.8 gather_fusion.1
  301.5 11.8 gather_fusion.2
  313.3 11.8 gather_fusion.3
  325.1 11.8 gather_fusion.4
  336.9 11.8 gather_fusion.5
  348.7 11.8 gather_fusion.6
  360.5 11.8 gather_fusion.7
  372.3 11.8 gather_fusion.8
  384.1 11.8 gather_fusion.9
  395.9 11.8 gather_fusion.10
  441.6 268.1 %collective-permute-done.1 = bf16[2048,5120]{1,0:T(8,128)(2,1)} collective-permute-done((bf16[2048,5120]{1,0:T(8,128)(2,1)}, bf16[2048,5120]{1,0:T(8,128)(2,1)}, u32[]{:S(2)}, u32[]{:S(2)}) %collective-permute-start.1) | collective-permute-done | bytes 20971552 | tf_op jit(solution)/shard_map/ppermute | solution.py:11
  709.7 38.8 %fusion.9 = f32[256,2048]{0,1:T(8,128)} fusion(bf16[256,10240]{1,0:T(8,128)(2,1)} %all-gather.2.cloned.1.call-done, bf16[2048,5120]{1,0:T(8,128)(2,1)} %collective-permute-done.1, bf16[2048,5120]{1,0:T(8,128)(2,1)} %maximum_select_fusion.2, f32[10240]{0:T(1024)S(1)} %multiply_exponential_fusion, pred[]{:T(512)S(6)} %eq.250, s32[256,2048]{0,1:T(8,128)S(1)} %copy-done.2, ...), kind=kOutput, calls=%fused_computation.40 | convolution fusion | flops 10991173632 | bytes 51422208 | tf_op jit(solution)/shard_map/dot_general | solution.py:65
  754.1 11.8 gather_fusion.11
  765.9 11.8 gather_fusion.13
  780.9 59.8 %collective-permute-done.2 = f32[256,2048]{0,1:T(8,128)} collective-permute-done((f32[256,2048]{0,1:T(8,128)}, f32[256,2048]{0,1:T(8,128)}, u32[]{:S(2)}, u32[]{:S(2)}) %collective-permute-start.2) | collective-permute-done | bytes 2097184 | tf_op jit(solution)/shard_map/ppermute | solution.py:22
  840.7 3.5 multiply_subtract_fusion.12
  844.5 11.8 gather_fusion.12
  856.4 3.1 fusion.63
  859.5 3.5 collective-permute-start.7
  863.1 49.2 %collective-permute-done.7 = bf16[256,2048]{0,1:T(8,128)(2,1)S(1)} collective-permute-done((bf16[256,2048]{0,1:T(8,128)(2,1)S(1)}, bf16[256,2048]{0,1:T(8,128)(2,1)S(1)}, u32[]{:S(2)}, u32[]{:S(2)}) %collective-permute-start.7) | collective-permute-done | bytes 1048608 | tf_op jit(solution)/shard_map/ppermute | solution.py:22
  912.3 4.5 collective-permute-done.3
  916.7 8.8 multiply_reduce_fusion
  927.6 14.7 %scatter_custom_fusion.12 = f32[8192]{0:T(1024)S(1)} fusion(s32[2048]{0:T(1024)S(1)} %bitcast.90, f32[2048]{0:T(1024)S(1)} %get-tuple-element.8, f32[]{:T(128)} %constant.42.clone.1), kind=kCustom, calls=%fused_computation.187 | custom fusion | flops 2048 | bytes 32772 | tf_op jit(solution)/shard_map/scatter-add | solution.py:49
  942.3 14.7 %scatter_custom_fusion.13 = f32[8192]{0:T(1024)S(1)} fusion(s32[2048]{0:T(1024)S(1)} %bitcast.89, f32[2048]{0:T(1024)S(1)} %get-tuple-element.7, f32[]{:T(128)} %constant.42.clone.1), kind=kCustom, calls=%fused_computation.185 | custom fusion | flops 2048 | bytes 32772 | tf_op jit(solution)/shard_map/scatter-add | solution.py:49
  957.0 15.1 %scatter_custom_fusion.11 = f32[8192]{0:T(1024)S(1)} fusion(s32[2048]{0:T(1024)S(1)} %bitcast.88, f32[2048]{0:T(1024)} %get-tuple-element.9, f32[]{:T(128)} %constant.42.clone.1), kind=kCustom, calls=%fused_computation.189 | custom fusion | flops 2048 | bytes 33280 | tf_op jit(solution)/shard_map/scatter-add | solution.py:49
  972.1 4.6 multiply_reduce_fusion.1
  977.1 4.0 multiply_reduce_fusion.2
  981.7 3.9 multiply_reduce_fusion.3
  988.7 3.4 multiply_reduce_fusion.4
  1027.2 3.2 multiply_reduce_fusion.10
  1034.1 3.2 fusion.62
  1037.3 14.9 %scatter_custom_fusion = f32[8192]{0:T(1024)S(1)} fusion(s32[2048]{0:T(1024)} %bitcast.87, f32[2048]{0:T(1024)S(1)} %get-tuple-element.33, f32[]{:T(128)} %constant.42.clone.1), kind=kCustom, calls=%fused_computation.211 | custom fusion | flops 2048 | bytes 33280 | tf_op jit(solution)/shard_map/scatter-add | solution.py:49
  1052.2 14.7 %scatter_custom_fusion.1 = f32[8192]{0:T(1024)S(1)} fusion(s32[2048]{0:T(1024)S(1)} %bitcast.86, f32[2048]{0:T(1024)S(1)} %get-tuple-element.31, f32[]{:T(128)} %constant.42.clone.1), kind=kCustom, calls=%fused_computation.209 | custom fusion | flops 2048 | bytes 32772 | tf_op jit(solution)/shard_map/scatter-add | solution.py:49
  1066.9 14.7 %scatter_custom_fusion.2 = f32[8192]{0:T(1024)S(1)} fusion(s32[2048]{0:T(1024)S(1)} %bitcast.85, f32[2048]{0:T(1024)S(1)} %get-tuple-element.29, f32[]{:T(128)} %constant.42.clone.1), kind=kCustom, calls=%fused_computation.207 | custom fusion | flops 2048 | bytes 32772 | tf_op jit(solution)/shard_map/scatter-add | solution.py:49
  1081.7 15.0 %scatter_custom_fusion.3 = f32[8192]{0:T(1024)S(1)} fusion(s32[2048]{0:T(1024)S(1)} %bitcast.84, f32[2048]{0:T(1024)S(1)} %get-tuple-element.27, f32[]{:T(128)} %constant.42.clone.1), kind=kCustom, calls=%fused_computation.205 | custom fusion | flops 2048 | bytes 32772 | tf_op jit(solution)/shard_map/scatter-add | solution.py:49
  1096.6 14.7 %scatter_custom_fusion.4 = f32[8192]{0:T(1024)S(1)} fusion(s32[2048]{0:T(1024)S(1)} %bitcast.83, f32[2048]{0:T(1024)S(1)} %get-tuple-element.25, f32[]{:T(128)} %constant.42.clone.1), kind=kCustom, calls=%fused_computation.203 | custom fusion | flops 2048 | bytes 32772 | tf_op jit(solution)/shard_map/scatter-add | solution.py:49
  1111.3 14.7 %scatter_custom_fusion.5 = f32[8192]{0:T(1024)S(1)} fusion(s32[2048]{0:T(1024)S(1)} %bitcast.82, f32[2048]{0:T(1024)S(1)} %get-tuple-element.23, f32[]{:T(128)} %constant.42.clone.1), kind=kCustom, calls=%fused_computation.201 | custom fusion | flops 2048 | bytes 32772 | tf_op jit(solution)/shard_map/scatter-add | solution.py:49
  1126.1 14.7 %scatter_custom_fusion.6 = f32[8192]{0:T(1024)S(1)} fusion(s32[2048]{0:T(1024)S(1)} %bitcast.81, f32[2048]{0:T(1024)S(1)} %get-tuple-element.21, f32[]{:T(128)} %constant.42.clone.1), kind=kCustom, calls=%fused_computation.199 | custom fusion | flops 2048 | bytes 32772 | tf_op jit(solution)/shard_map/scatter-add | solution.py:49
  1140.8 14.7 %scatter_custom_fusion.7 = f32[8192]{0:T(1024)S(1)} fusion(s32[2048]{0:T(1024)S(1)} %bitcast.80, f32[2048]{0:T(1024)S(1)} %get-tuple-element.19, f32[]{:T(128)} %constant.42.clone.1), kind=kCustom, calls=%fused_computation.197 | custom fusion | flops 2048 | bytes 32772 | tf_op jit(solution)/shard_map/scatter-add | solution.py:49
  1155.5 14.7 %scatter_custom_fusion.8 = f32[8192]{0:T(1024)S(1)} fusion(s32[2048]{0:T(1024)S(1)} %bitcast.79, f32[2048]{0:T(1024)S(1)} %get-tuple-element.17, f32[]{:T(128)} %constant.42.clone.1), kind=kCustom, calls=%fused_computation.195 | custom fusion | flops 2048 | bytes 32772 | tf_op jit(solution)/shard_map/scatter-add | solution.py:49
  1170.2 14.7 %scatter_custom_fusion.9 = f32[8192]{0:T(1024)S(1)} fusion(s32[2048]{0:T(1024)S(1)} %bitcast.78, f32[2048]{0:T(1024)S(1)} %get-tuple-element.15, f32[]{:T(128)} %constant.42.clone.1), kind=kCustom, calls=%fused_computation.193 | custom fusion | flops 2048 | bytes 32772 | tf_op jit(solution)/shard_map/scatter-add | solution.py:49
  1185.0 14.7 %scatter_custom_fusion.10 = f32[8192]{0:T(1024)S(1)} fusion(s32[2048]{0:T(1024)S(1)} %bitcast.77, f32[2048]{0:T(1024)S(1)} %get-tuple-element.13, f32[]{:T(128)} %constant.42.clone.1), kind=kCustom, calls=%fused_computation.191 | custom fusion | flops 2048 | bytes 32772 | tf_op jit(solution)/shard_map/scatter-add | solution.py:49
  1206.0 27.1 %reduce-scatter.2.cloned.1.call-done = f32[14,1024]{1,0:T(8,128)} async-done(((f32[14,8192]{1,0:T(8,128)}), f32[14,1024]{1,0:T(8,128)}) %reduce-scatter.2.cloned.1.call-update) | async-done | bytes 57360 | tf_op jit(solution)/shard_map/reduce_scatter | solution.py:99
  1233.0 18.0 %psum.7 = f32[14,1024]{1,0:T(8,128)} all-reduce(f32[14,1024]{1,0:T(8,128)} %reduce-scatter.2.cloned.1.call-done), channel_id=1, replica_groups=mesh['dp'=4,'tensor'=8] {'dp'}, use_global_device_ids=true, to_apply=%region_29.31 | all-reduce | flops 14336 | bytes 114688 | tf_op jit(solution)/shard_map/psum | solution.py:100
  (242 shorter events, 99.7 us)
Async XLA Ops:
  7.2 434.4 %all-gather.2.cloned.1.call-start = ((), (), s32[]{:S(2)}) async-start(), calls=%async_computation.1 | async-start | bytes 5898240 | tf_op jit(solution)/shard_map/all_gather | solution.py:61
  7.2 228.7 %collective-permute-start = (bf16[2048,2560]{1,0:T(8,128)(2,1)}, bf16[2048,2560]{1,0:T(8,128)(2,1)}, u32[]{:S(2)}, u32[]{:S(2)}) collective-permute-start(bf16[2048,2560]{1,0:T(8,128)(2,1)} %param.11), channel_id=1, source_target_pairs={{0,8},{8,0},{16,24},{24,16},{1,9},{9,1},{17,25},{25,17},{2,10},{10... | collective-permute-start | bytes 31457288 | tf_op jit(solution)/shard_map/ppermute | solution.py:11
  10.2 249.7 %copy-start.3 = (bf16[256,2048]{1,0:T(8,128)(2,1)S(1)}, bf16[256,2048]{1,0:T(8,128)(2,1)}, u32[]{:S(2)}) copy-start(bf16[256,2048]{1,0:T(8,128)(2,1)} %param.8) | copy-start | bytes 3145732
  258.0 2.5 copy-start.29
  258.0 451.6 %collective-permute-start.1 = (bf16[2048,5120]{1,0:T(8,128)(2,1)}, bf16[2048,5120]{1,0:T(8,128)(2,1)}, u32[]{:S(2)}, u32[]{:S(2)}) collective-permute-start(bf16[2048,5120]{1,0:T(8,128)(2,1)} %maximum_select_fusion.2), channel_id=1, source_target_pairs={{0,16},{8,24},{16,0},{24,8},{1,17},{9,25},{17,1},{25,9},{2,18},{10... | collective-permute-start | bytes 62914568 | tf_op jit(solution)/shard_map/ppermute | solution.py:11
  259.9 973.1 %reduce-scatter.2.cloned.1.call-start = ((), (), s32[]{:S(2)}) async-start(), calls=%async_computation.2 | async-start | bytes 589824 | tf_op jit(solution)/shard_map/reduce_scatter | solution.py:99
  407.7 3.4 copy-start.30
  407.8 6.3 copy-start.38
  407.8 9.6 copy-start.32
  407.8 16.5 %copy-start.34 = (pred[2048]{0:T(1024)(128)(4,1)}, pred[2048]{0:T(1024)(128)(4,1)S(1)}, u32[]{:S(2)}) copy-start(pred[2048]{0:T(1024)(128)(4,1)S(1)} %get-tuple-element.245) | copy-start | bytes 6148
  407.8 18.9 %copy-start.36 = (pred[2048]{0:T(1024)(128)(4,1)}, pred[2048]{0:T(1024)(128)(4,1)S(1)}, u32[]{:S(2)}) copy-start(pred[2048]{0:T(1024)(128)(4,1)S(1)} %get-tuple-element.246) | copy-start | bytes 6148
  407.9 0.6 copy-start.25
  410.8 0.6 copy-start.17
  416.6 0.8 copy-start.4
  416.6 0.8 copy-start.6
  416.6 7.6 copy-start.9
  416.7 7.6 copy-start.11
  416.7 9.9 copy-start.13
  416.7 9.9 copy-start.15
  417.4 2.0 copy-start.8
  439.9 1.7 copy-start.1
  439.9 1.6 copy-start.40
  439.9 269.8 %copy-start.2 = (s32[256,2048]{0,1:T(8,128)S(1)}, s32[256,2048]{0,1:T(8,128)}, u32[]{:S(2)}) copy-start(s32[256,2048]{0,1:T(8,128)} %copy.11) | copy-start | bytes 6291460
  748.5 92.2 %collective-permute-start.2 = (f32[256,2048]{0,1:T(8,128)}, f32[256,2048]{0,1:T(8,128)}, u32[]{:S(2)}, u32[]{:S(2)}) collective-permute-start(f32[256,2048]{0,1:T(8,128)} %fusion.9), channel_id=1, source_target_pairs={{0,4},{1,5},{2,6},{3,7},{4,0},{5,1},{6,2},{7,3},{8,12},{9,13},{10,... | collective-permute-start | bytes 6291464 | tf_op jit(solution)/shard_map/ppermute | solution.py:22
  754.1 23.7 %collective-permute-start.5 = (bf16[256,2048]{0,1:T(8,128)(2,1)}, bf16[256,2048]{0,1:T(8,128)(2,1)S(1)}, u32[]{:S(2)}, u32[]{:S(2)}) collective-permute-start(bf16[256,2048]{0,1:T(8,128)(2,1)} %get-tuple-element.11), channel_id=1, source_target_pairs={{0,1},{1,0},{2,3},{3,2},{4,5},{5,4},{6,7},{7,6},{8,9},{9,8},{10,11... | collective-permute-start | bytes 3145736 | tf_op jit(solution)/shard_map/ppermute | solution.py:22
  779.3 77.1 %collective-permute-start.6 = (bf16[256,2048]{0,1:T(8,128)(2,1)}, bf16[256,2048]{0,1:T(8,128)(2,1)}, u32[]{:S(2)}, u32[]{:S(2)}) collective-permute-start(bf16[256,2048]{0,1:T(8,128)(2,1)} %fusion.189), channel_id=1, source_target_pairs={{0,2},{1,3},{2,0},{3,1},{4,6},{5,7},{6,4},{7,5},{8,10},{9,11},{10,... | collective-permute-start | bytes 3145736 | tf_op jit(solution)/shard_map/ppermute | solution.py:22
  840.7 3.8 copy-start
  844.2 72.5 %collective-permute-start.3 = (f32[256,2048]{0,1:T(8,128)}, f32[256,2048]{0,1:T(8,128)}, u32[]{:S(2)}, u32[]{:S(2)}) collective-permute-start(f32[256,2048]{0,1:T(8,128)} %multiply_subtract_fusion.12), channel_id=1, source_target_pairs={{0,2},{1,3},{2,0},{3,1},{4,6},{5,7},{6,4},{7,5},{8,10},{9,11},{10,... | collective-permute-start | bytes 6291464 | tf_op jit(solution)/shard_map/ppermute | solution.py:22
  859.5 52.8 %collective-permute-start.7 = (bf16[256,2048]{0,1:T(8,128)(2,1)S(1)}, bf16[256,2048]{0,1:T(8,128)(2,1)S(1)}, u32[]{:S(2)}, u32[]{:S(2)}) collective-permute-start(bf16[256,2048]{0,1:T(8,128)(2,1)S(1)} %fusion.63), channel_id=1, source_target_pairs={{0,4},{1,5},{2,6},{3,7},{4,0},{5,1},{6,2},{7,3},{8,12},{9,13},{10,... | collective-permute-start | bytes 3145736 | tf_op jit(solution)/shard_map/ppermute | solution.py:22
  925.5 46.5 %collective-permute-start.4 = (f32[256,2048]{0,1:T(8,128)}, f32[256,2048]{0,1:T(8,128)}, u32[]{:S(2)}, u32[]{:S(2)}) collective-permute-start(f32[256,2048]{0,1:T(8,128)} %get-tuple-element.10), channel_id=1, source_target_pairs={{0,1},{1,0},{2,3},{3,2},{4,5},{5,4},{6,7},{7,6},{8,9},{9,8},{10,11... | collective-permute-start | bytes 6291464 | tf_op jit(solution)/shard_map/ppermute | solution.py:22
  1000.7 0.7 copy-start.37
  1004.4 0.7 copy-start.14
  1004.4 0.7 copy-start.16
  1007.2 0.7 copy-start.35
  1010.8 0.7 copy-start.10
  1010.8 0.7 copy-start.12
  1013.7 0.7 copy-start.33
  1017.2 0.7 copy-start.5
  1017.2 0.7 copy-start.7
  1019.8 0.7 copy-start.39
  1023.4 0.7 copy-start.22
  1023.4 0.7 copy-start.24
  1026.5 0.7 copy-start.31
  1030.4 0.7 copy-start.18
  1030.4 0.7 copy-start.20
  1033.4 0.7 copy-start.42
  1201.8 0.7 copy-start.26
  1201.8 0.7 copy-start.28
  (5 other events, 3.0 us)
Sparse Core Ops, SparseCore 0:
  260.0 57.4 all-gather.1
  1201.9 31.1 reduce-scatter.1
